TPU v7x, 512 devices: a whole 4x4x16 slice. The times are simulated.
512 devices in a mesh: seq: 64 (over y_lo, z, core), tensor: 8 (over x, y_hi).
Axes of the slice: x: 4, y: 4 (y_hi: 2, y_lo: 2; y = y_hi * 2 + y_lo), z: 16, core: 2. Of those that a mesh axis runs over, the one named last changes fastest.
Arguments:
- trunk: bfloat16 [2, 4096, 1536], P(None, 'seq', 'tensor'), may hold values from -12 to 12
- w_out: bfloat16 [1536, 1536], P('tensor', 'seq'), may hold values from -1 to 1
- gain_coarse: float32 [1536], replicated, may hold values from 0.1 to 1.9
- w_conv1: bfloat16 [5, 1536, 1536], P(None, 'seq', 'tensor'), may hold values from -0.0625 to 0.0625
- w_up: bfloat16 [1536, 2, 768], P('seq', None, 'tensor'), may hold values from -0.15625 to 0.15625
- skip: bfloat16 [2, 8192, 768], P(None, 'seq', 'tensor'), may hold values from -12 to 12
- gain_fine: float32 [768], replicated, may hold values from 0.1 to 1.9
- w_conv2: bfloat16 [5, 768, 768], P(None, 'seq', 'tensor'), may hold values from -0.09375 to 0.09375
- cotangent: bfloat16 [2, 8192, 768], P(None, 'seq', 'tensor'), may hold values from -6 to 6
Outputs:
- decoded: bfloat16 [2, 8192, 768], P(None, 'seq', 'tensor')
- skip_grad: bfloat16 [2, 8192, 768], P(None, 'seq', 'tensor')
- trunk_grad: bfloat16 [2, 4096, 1536], P(None, 'seq', 'tensor')
All inputs are finite; a program needn't handle non-finite values.
Results may differ from a plain program's by a relative error of at most 0.02.
Values may be sent and summed in bfloat16 or wider, within the bound.
No kernel may reach another device: no remote copies, remote signals or barrier semaphores. Data moves between devices by JAX's collectives and lax.ppermute only.
A program may use at most 64 MiB of HBM per device.

v0:
```python
import jax
import jax.numpy as jnp
from jax import lax
from jax.sharding import PartitionSpec as P

C_COARSE = 1536
C_FINE = 768
EPS = 1e-06


def extended(shard, sides, width):
    for axis, dim in sides:
        size, length = (lax.axis_size(axis), shard.shape[dim])
        up = [(i, (i + 1) % size) for i in range(size - 1)]
        down = [(j, i) for i, j in up]
        last = lax.slice_in_dim(shard, length - width, length, axis=dim)
        leading = lax.slice_in_dim(shard, 0, width, axis=dim)
        before = lax.ppermute(last, axis, up)
        after = lax.ppermute(leading, axis, down)
        shard = jnp.concatenate([before, shard, after], axis=dim)
    return shard


def matmul(left, right):
    return lax.dot_general(
        left, right, (((left.ndim - 1,), (0,)), ((), ())), preferred_element_type=jnp.float32
    )


def matmul_back(left, right):
    return lax.dot_general(
        left,
        right,
        (((left.ndim - 1,), (right.ndim - 1,)), ((), ())),
        preferred_element_type=jnp.float32,
    )


def activate(field, gain):
    scaled = field * lax.rsqrt(jnp.mean(field * field, axis=-1, keepdims=True) + EPS)
    return jax.nn.gelu(scaled * gain)


def widen(field):
    return extended(field, (("seq", 1),), 2)


def spread(field):
    return lax.all_gather(field, "tensor", axis=2, tiled=True)


def conv_rows(total, wide, piece):
    length = wide.shape[1] - 4
    for k in range(5):
        total = total + matmul(wide[:, k : k + length], piece[k])
    return total


def conv_back(wide_grad, piece):
    length = wide_grad.shape[1] - 4
    total = jnp.zeros((wide_grad.shape[0], length, piece.shape[1]), jnp.float32)
    for k in range(5):
        total = total + matmul_back(wide_grad[:, 4 - k : 4 - k + length], piece[k])
    return total


def norm_back(partial_grad, field_full, gain, rank, part):
    field = field_full.astype(jnp.float32)
    start = rank * part
    whole = lax.psum(partial_grad.astype(jnp.bfloat16), "tensor").astype(jnp.float32)

    def apply(value):
        return activate(value, gain)

    _, pull = jax.vjp(apply, field)
    return lax.dynamic_slice_in_dim(pull(whole)[0], start, part, 2)


def per_device(trunk, w_out, gain_coarse, w_conv1, w_up, skip, gain_fine, w_conv2, cotangent):
    rank = lax.axis_index("tensor")
    part_coarse = C_COARSE // lax.axis_size("tensor")
    part_fine = C_FINE // lax.axis_size("tensor")
    seqs = trunk.shape[0]
    slab = trunk.shape[1]
    out_w, up_w, conv2_w = (
        lax.all_gather(w_out, "seq", axis=1, tiled=True),
        lax.all_gather(w_up, "seq", axis=0, tiled=True),
        lax.all_gather(w_conv2, "seq", axis=1, tiled=True),
    )
    partial_proj = matmul(trunk, out_w)
    projected = lax.psum_scatter(
        partial_proj.astype(jnp.bfloat16), "tensor", scatter_dimension=2, tiled=True
    )
    projected_full = lax.all_gather(projected, "tensor", axis=2, tiled=True)
    act_coarse = activate(projected_full.astype(jnp.float32), gain_coarse).astype(jnp.bfloat16)
    coarse_wide = widen(act_coarse)
    empty_coarse = jnp.zeros((seqs, slab, part_coarse), jnp.float32)
    mixed_coarse = conv_rows(
        empty_coarse, coarse_wide, lax.all_gather(w_conv1, "seq", axis=1, tiled=True)
    )
    lifted = (projected.astype(jnp.float32) + mixed_coarse).astype(jnp.bfloat16)
    lifted_full = spread(lifted)
    upper = matmul(lifted_full, up_w).reshape(seqs, 2 * slab, part_fine)
    merged = (upper + skip.astype(jnp.float32)).astype(jnp.bfloat16)
    merged_full = spread(merged)
    act_fine = activate(merged_full.astype(jnp.float32), gain_fine).astype(jnp.bfloat16)
    fine_wide = widen(act_fine)
    empty_fine = jnp.zeros((seqs, 2 * slab, part_fine), jnp.float32)
    mixed_fine = conv_rows(empty_fine, fine_wide, conv2_w)
    decoded = (merged.astype(jnp.float32) + mixed_fine).astype(jnp.bfloat16)
    cot_wide = widen(cotangent)
    back_fine = conv_back(cot_wide, conv2_w)
    skip_grad = (
        cotangent.astype(jnp.float32)
        + norm_back(back_fine, merged_full, gain_fine, rank, part_fine)
    ).astype(jnp.bfloat16)
    folded = skip_grad.reshape(seqs, slab, 2 * part_fine)
    up_partial = matmul_back(folded, up_w.reshape(up_w.shape[0], 2 * part_fine))
    lifted_grad = lax.psum_scatter(
        up_partial.astype(jnp.bfloat16), "tensor", scatter_dimension=2, tiled=True
    )
    grad_wide = widen(lifted_grad)
    back_coarse = conv_back(grad_wide, lax.all_gather(w_conv1, "seq", axis=1, tiled=True))
    projected_grad = (
        lifted_grad.astype(jnp.float32)
        + norm_back(back_coarse, projected_full, gain_coarse, rank, part_coarse)
    ).astype(jnp.bfloat16)
    grad_full = spread(projected_grad)
    trunk_grad = matmul_back(grad_full, out_w).astype(jnp.bfloat16)
    return (decoded, skip_grad, trunk_grad)


def solution(mesh):
    in_specs = (
        P(None, "seq", "tensor"),
        P("tensor", "seq"),
        P(),
        P(None, "seq", "tensor"),
        P("seq", None, "tensor"),
        P(None, "seq", "tensor"),
        P(),
        P(None, "seq", "tensor"),
        P(None, "seq", "tensor"),
    )
    out_specs = (P(None, "seq", "tensor"), P(None, "seq", "tensor"), P(None, "seq", "tensor"))
    return jax.shard_map(
        per_device, mesh=mesh, in_specs=in_specs, out_specs=out_specs, check_vma=False
    )
```

profile of v0, /device:TPU:32, one launch (start us, length us, event | category | flops | bytes accessed | tf_op | source)
XLA Modules:
  0.0 605.8 jit_solution(13952073995251404903)
XLA Ops:
  8.1 69.1 %all_gather.25 = bf16[192,1536]{0,1:T(8,128)(2,1)S(1)} all-gather(bf16[192,24]{0,1:T(8,128)(2,1)} %param.10), channel_id=1, replica_groups=mesh['seq'=64,'tensor'=8] {'seq'}, dimensions={1}, use_global_device_ids=true | all-gather | bytes 599040 | tf_op jit(solution)/shard_map/all_gather | solution.py:86
  78.1 1.1 reshape.66
  80.6 5.0 collective-permute-start.4
  85.6 1.9 collective-permute-start.5
  88.9 65.4 %all_gather.31 = bf16[5,768,96]{2,0,1:T(8,128)(2,1)S(1)} all-gather(bf16[5,12,96]{2,0,1:T(8,128)(2,1)S(1)} %copy.52), channel_id=1, replica_groups=mesh['seq'=64,'tensor'=8] {'seq'}, dimensions={1}, use_global_device_ids=true | all-gather | bytes 748800 | tf_op jit(solution)/shard_map/all_gather | solution.py:88
  154.3 1.4 fusion.107
  155.8 0.9 copy.76
  157.0 0.9 copy.75
  158.8 0.9 copy.78
  160.6 62.1 %all_gather.29 = bf16[1536,2,96]{2,0,1:T(8,128)(2,1)S(1)} all-gather(bf16[24,2,96]{2,0,1:T(8,128)(2,1)} %copy.46), channel_id=1, replica_groups=mesh['seq'=64,'tensor'=8] {'seq'}, dimensions={0}, use_global_device_ids=true | all-gather | bytes 599040 | tf_op jit(solution)/shard_map/all_gather | solution.py:87
  223.0 1.4 constant_dynamic-update-slice_fusion
  224.4 1.3 fusion.60
  225.7 1.3 fusion.69
  227.1 1.3 fusion.4
  228.3 1.9 fusion.5
  231.3 37.2 %all_gather.26 = bf16[2,64,1536]{1,0,2:T(2,128)(2,1)S(1)} all-gather(bf16[2,64,192]{1,0,2:T(2,128)(2,1)S(1)} %bitcast.93), channel_id=1, replica_groups=mesh['seq'=64,'tensor'=8] {'tensor'}, dimensions={2}, use_global_device_ids=true | all-gather | bytes 442368 | tf_op jit(solution)/shard_map/all_gather | solution.py:94
  269.9 1.0 convert_element_type.67
  271.4 1.1 multiply_convert_fusion.1
  272.6 1.9 collective-permute-start
  274.5 3.6 collective-permute-start.1
  278.2 1.4 fusion.43
  279.6 1.4 fusion.41
  281.0 1.4 fusion.45
  282.5 1.4 fusion.6
  283.9 1.4 fusion.9
  285.5 35.9 %all_gather.28 = bf16[2,64,1536]{1,0,2:T(2,128)(2,1)S(1)} all-gather(bf16[2,64,192]{1,0,2:T(2,128)(2,1)S(1)} %copy.45), channel_id=1, replica_groups=mesh['seq'=64,'tensor'=8] {'tensor'}, dimensions={2}, use_global_device_ids=true | all-gather | bytes 442368 | tf_op jit(solution)/shard_map/all_gather | solution.py:49
  322.6 34.9 %all_gather.30 = bf16[2,128,768]{1,0,2:T(2,128)(2,1)S(1)} all-gather(bf16[2,128,96]{1,0,2:T(2,128)(2,1)S(1)} %copy.50), channel_id=1, replica_groups=mesh['seq'=64,'tensor'=8] {'tensor'}, dimensions={2}, use_global_device_ids=true | all-gather | bytes 442368 | tf_op jit(solution)/shard_map/all_gather | solution.py:49
  358.8 1.9 multiply_reduce_fusion.1
  361.4 1.0 fusion.75
  363.9 1.1 reshape.68
  365.2 1.9 collective-permute-start.2
  367.4 1.6 copy.62
  368.9 3.6 collective-permute-start.3
  372.6 1.2 fusion.56
  373.8 1.2 fusion.10
  375.0 69.0 %reduce-scatter.9.cloned.1.call-done = bf16[192,128]{1,0:T(8,128)(2,1)} async-done(((bf16[1536,128]{1,0:T(8,128)(2,1)}), bf16[192,128]{1,0:T(8,128)(2,1)}) %reduce-scatter.9.cloned.1.call-update) | async-done | bytes 49168
  445.0 1.9 collective-permute-start.6
  447.0 2.6 collective-permute-start.7
  449.5 1.5 fusion.42
  451.1 1.5 fusion.40
  452.6 1.6 fusion.44
  454.2 1.6 fusion
  455.9 2.3 fusion.2
  459.4 99.1 %all-reduce.5.cloned.1.call-done = bf16[2,64,1536]{2,1,0:T(8,128)(2,1)} async-done(((bf16[2,64,1536]{2,1,0:T(8,128)(2,1)}), bf16[2,64,1536]{2,1,0:T(8,128)(2,1)}) %all-reduce.5.cloned.1.call-update) | async-done | bytes 393232 | tf_op jit(solution)/shard_map/psum | solution.py:70
  558.5 1.8 multiply_reduce_fusion
  560.3 1.1 fusion.77
  561.6 36.0 %all_gather.32 = bf16[2,64,1536]{1,0,2:T(2,128)(2,1)S(1)} all-gather(bf16[2,64,192]{1,0,2:T(2,128)(2,1)S(1)} %copy.60), channel_id=1, replica_groups=mesh['seq'=64,'tensor'=8] {'tensor'}, dimensions={2}, use_global_device_ids=true | all-gather | bytes 442368 | tf_op jit(solution)/shard_map/all_gather | solution.py:49
  597.6 1.1 convolution_convert_fusion.2
  (99 shorter events, 16.5 us)
Async XLA Ops:
  8.0 69.1 %copy-start = (bf16[2,64,192]{2,1,0:T(8,128)(2,1)S(1)}, bf16[2,64,192]{2,1,0:T(8,128)(2,1)}, u32[]{:S(2)}) copy-start(bf16[2,64,192]{2,1,0:T(8,128)(2,1)} %param.9) | copy-start | bytes 147460
  8.0 71.9 %copy-start.1 = (bf16[2,128,96]{1,2,0:T(8,128)(2,1)S(1)}, bf16[2,128,96]{1,2,0:T(8,128)(2,1)}, u32[]{:S(2)}) copy-start(bf16[2,128,96]{1,2,0:T(8,128)(2,1)} %param.17) | copy-start | bytes 147460
  8.0 80.3 %copy-start.15 = (bf16[24,2,96]{2,1,0:T(2,128)(2,1)S(1)}, bf16[24,2,96]{2,1,0:T(2,128)(2,1)}, u32[]{:S(2)}) copy-start(bf16[24,2,96]{2,1,0:T(2,128)(2,1)} %param.13) | copy-start | bytes 27652
  8.0 80.9 %copy-start.12 = (bf16[5,12,96]{2,1,0:T(8,128)(2,1)S(1)}, bf16[5,12,96]{2,1,0:T(8,128)(2,1)}, u32[]{:S(2)}) copy-start(bf16[5,12,96]{2,1,0:T(8,128)(2,1)} %param.16) | copy-start | bytes 34564
  8.0 222.3 %reduce-scatter.7.cloned.1.call-start = ((), (), s32[]{:S(2)}) async-start(), calls=%async_computation.5 | async-start | bytes 442368
  79.3 198.9 %all-gather.2.cloned.1.call-start = ((), (), s32[]{:S(2)}) async-start(), calls=%async_computation.2 | async-start | bytes 3993600 | tf_op jit(solution)/shard_map/all_gather | solution.py:99
  79.8 278.9 %all-reduce.3.cloned.1.call-start = ((), (), s32[]{:S(2)}) async-start(), calls=%async_computation.3 | async-start | bytes 786432 | tf_op jit(solution)/shard_map/psum | solution.py:70
  80.6 142.4 %collective-permute-start.4 = (bf16[2,2,96]{1,2,0:T(8,128)(2,1)}, bf16[2,2,96]{1,2,0:T(8,128)(2,1)}, u32[]{:S(2)}, u32[]{:S(2)}) collective-permute-start(bf16[2,2,96]{1,2,0:T(8,128)(2,1)} %get-tuple-element.28), channel_id=1, source_target_pairs={{8,0},{16,8},{24,16},{32,24},{40,32},{48,40},{56,48},{64,56},{72,6... | collective-permute-start | bytes 2312 | tf_op jit(solution)/shard_map/ppermute | solution.py:19
  85.6 138.8 %collective-permute-start.5 = (bf16[2,2,96]{1,2,0:T(8,128)(2,1)}, bf16[2,2,96]{1,2,0:T(8,128)(2,1)}, u32[]{:S(2)}, u32[]{:S(2)}) collective-permute-start(bf16[2,2,96]{1,2,0:T(8,128)(2,1)} %get-tuple-element.29), channel_id=1, source_target_pairs={{0,8},{8,16},{16,24},{24,32},{32,40},{40,48},{48,56},{56,64},{64,7... | collective-permute-start | bytes 2312 | tf_op jit(solution)/shard_map/ppermute | solution.py:18
  159.7 67.3 %copy-start.4 = (bf16[1,768,96]{1,2,0:T(8,128)(2,1)S(1)}, bf16[1,768,96]{1,2,0:T(8,128)(2,1)}, u32[]{:S(2)}) copy-start(bf16[1,768,96]{1,2,0:T(8,128)(2,1)} %copy.75) | copy-start | bytes 442372
  160.4 68.0 %copy-start.2 = (bf16[1,768,96]{1,2,0:T(8,128)(2,1)S(1)}, bf16[1,768,96]{1,2,0:T(8,128)(2,1)}, u32[]{:S(2)}) copy-start(bf16[1,768,96]{1,2,0:T(8,128)(2,1)} %copy.78) | copy-start | bytes 442372
  230.3 213.7 %reduce-scatter.9.cloned.1.call-start = ((), (), s32[]{:S(2)}) async-start(), calls=%async_computation.6 | async-start | bytes 442368
  269.9 4.6 copy-start.16
  270.9 0.5 copy-start.13
  271.4 12.5 %copy-start.9 = (bf16[2,64,192]{2,1,0:T(8,128)(2,1)S(1)}, bf16[2,64,192]{2,1,0:T(8,128)(2,1)}, u32[]{:S(2)}) copy-start(bf16[2,64,192]{2,1,0:T(8,128)(2,1)} %copy.67) | copy-start | bytes 147460
  272.6 7.0 %collective-permute-start = (bf16[2,2,1536]{2,1,0:T(2,128)(2,1)S(1)}, bf16[2,2,1536]{2,1,0:T(2,128)(2,1)S(1)}, u32[]{:S(2)}, u32[]{:S(2)}) collective-permute-start(bf16[2,2,1536]{2,1,0:T(2,128)(2,1)S(1)} %get-tuple-element.24), channel_id=1, source_target_pairs={{0,8},{8,16},{16,24},{24,32},{32,40},{40,48},{48,56},{56,64},{64,7... | collective-permute-start | bytes 36872 | tf_op jit(solution)/shard_map/ppermute | solution.py:18
  274.5 6.5 %collective-permute-start.1 = (bf16[2,2,1536]{2,1,0:T(2,128)(2,1)S(1)}, bf16[2,2,1536]{2,1,0:T(2,128)(2,1)S(1)}, u32[]{:S(2)}, u32[]{:S(2)}) collective-permute-start(bf16[2,2,1536]{2,1,0:T(2,128)(2,1)S(1)} %get-tuple-element.25), channel_id=1, source_target_pairs={{8,0},{16,8},{24,16},{32,24},{40,32},{48,40},{56,48},{64,56},{72,6... | collective-permute-start | bytes 36872 | tf_op jit(solution)/shard_map/ppermute | solution.py:19
  282.5 39.5 %copy-start.10 = (bf16[2,128,96]{1,2,0:T(8,128)(2,1)S(1)}, bf16[2,128,96]{1,2,0:T(8,128)(2,1)}, u32[]{:S(2)}) copy-start(bf16[2,128,96]{1,2,0:T(8,128)(2,1)} %param.14) | copy-start | bytes 147460
  322.0 0.6 copy-start.7
  358.2 0.6 copy-start.18
  362.5 0.6 copy-start.5
  365.1 193.4 %all-reduce.5.cloned.1.call-start = ((), (), s32[]{:S(2)}) async-start(), calls=%async_computation.4 | async-start | bytes 786432 | tf_op jit(solution)/shard_map/psum | solution.py:70
  365.2 7.4 %collective-permute-start.2 = (bf16[2,2,768]{2,1,0:T(2,128)(2,1)S(1)}, bf16[2,2,768]{2,1,0:T(2,128)(2,1)S(1)}, u32[]{:S(2)}, u32[]{:S(2)}) collective-permute-start(bf16[2,2,768]{2,1,0:T(2,128)(2,1)S(1)} %get-tuple-element.22), channel_id=1, source_target_pairs={{0,8},{8,16},{16,24},{24,32},{32,40},{40,48},{48,56},{56,64},{64,7... | collective-permute-start | bytes 18440 | tf_op jit(solution)/shard_map/ppermute | solution.py:18
  368.9 89.3 %collective-permute-start.3 = (bf16[2,2,768]{2,1,0:T(2,128)(2,1)S(1)}, bf16[2,2,768]{2,1,0:T(2,128)(2,1)S(1)}, u32[]{:S(2)}, u32[]{:S(2)}) collective-permute-start(bf16[2,2,768]{2,1,0:T(2,128)(2,1)S(1)} %get-tuple-element.23), channel_id=1, source_target_pairs={{8,0},{16,8},{24,16},{32,24},{40,32},{48,40},{56,48},{64,56},{72,6... | collective-permute-start | bytes 18440 | tf_op jit(solution)/shard_map/ppermute | solution.py:19
  445.0 6.1 collective-permute-start.6
  447.0 5.7 collective-permute-start.7
  452.6 5.6 copy-start.6
  454.2 4.3 copy-start.3
  454.2 4.3 copy-start.8
  454.2 104.3 %copy-start.11 = (f32[1536]{0:T(1024)S(1)}, f32[1536]{0:T(1024)}, u32[]{:S(2)}) copy-start(f32[1536]{0:T(1024)} %param.11) | copy-start | bytes 18436
  454.2 104.3 %copy-start.14 = (f32[2,64]{1,0:T(2,128)S(1)}, f32[2,64]{1,0:T(2,128)}, u32[]{:S(2)}) copy-start(f32[2,64]{1,0:T(2,128)} %copy-done.13) | copy-start | bytes 1540
  455.8 104.5 %copy-start.17 = (f32[2,64]{1,0:T(2,128)S(1)}, f32[2,64]{1,0:T(2,128)}, u32[]{:S(2)}) copy-start(f32[2,64]{1,0:T(2,128)} %copy-done.16) | copy-start | bytes 1540
Sparse Core Ops, SparseCore 0:
  79.4 80.6 reduce-scatter.6
  230.4 92.9 all-reduce.2
  365.2 78.7 reduce-scatter.8
  458.3 100.1 all-reduce.4
Sparse Core Ops, SparseCore 1:
  81.8 117.8 all-gather.1
where the time goes:
time: 607 us; the launch traced here: 606 us
  blocking collectives  341 us (56%)
  waiting for transfers between devices  169 us (28%)
  matrix products  27.6 us (5%)
  starting transfers between devices  22.8 us (4%)
  local copies, waits for them, and re-layouts  20.7 us (3%)
  between operations  15.9 us (3%)
  other arithmetic  9.67 us (2%)
    all_gather x3, blocking collectives, spread(): return lax.all_gather(field, 'tensor', axis=2, tiled=True)  107 us
    psum x2, waiting for transfers between devices, norm_back(): lax.psum(partial_grad.astype(jnp.bfloat16), 'tensor').astype(jnp.float32)  99.1 us
    unnamed x7, waiting for transfers between devices  69.6 us
    all_gather x1, blocking collectives, per_device(): lax.all_gather(w_out, 'seq', axis=1, tiled=True)  69.1 us
    all_gather x1, blocking collectives, per_device(): lax.all_gather(w_conv2, 'seq', axis=1, tiled=True)  65.4 us
    all_gather x1, blocking collectives, per_device(): lax.all_gather(w_up, 'seq', axis=0, tiled=True)  62.1 us
    all_gather x1, blocking collectives, per_device(): projected_full = lax.all_gather(projected, 'tensor', axis=2, tiled=True)  37.2 us
    dot_general x12, matrix products, matmul_back(): lax.dot_general(left, right, (((left.ndim - 1,), (right.ndim - 1,)), ((),...  15.9 us
  transfers between devices with their start and end apart: 13, of which 2 were waited for; matrix products, arithmetic and copies ran while one was open for 7% of the time, Pallas kernels for 0%

commit v1 on v0

--- a/solution.py
+++ b/solution.py
@@ -67,7 +67,9 @@
 def norm_back(partial_grad, field_full, gain, rank, part):
     field = field_full.astype(jnp.float32)
     start = rank * part
-    whole = lax.psum(partial_grad.astype(jnp.bfloat16), "tensor").astype(jnp.float32)
+    whole = jnp.sum(lax.all_gather(partial_grad.astype(jnp.bfloat16), "tensor"), axis=0).astype(
+        jnp.float32
+    )
 
     def apply(value):
         return activate(value, gain)

time: 607 us -> 685 us (1.13)
  waiting for transfers between devices: 169 us -> 253 us
    all_gather x1, waiting for transfers between devices: 0.03 us -> 99.5 us  [per_device(): lax.all_gather(w_conv1, 'seq', axis=1, tiled=True)]
    psum x2 -> x0, waiting for transfers between devices: 99.1 us -> none  [norm_back(): lax.psum(partial_grad.astype(jnp.bfloat16), 'tensor').astype(jnp.float32)]
    all_gather x0 -> x2, waiting for transfers between devices: none -> 68.3 us  [norm_back(): lax.all_gather(partial_grad.astype(jnp.bfloat16), 'tensor')]
    unnamed x7, waiting for transfers between devices: 69.6 us -> 84.4 us
    unnamed x56 -> x60, local copies, waits for them, and re-layouts: 15.2 us -> 11.7 us
  transfers between devices with their start and end apart: 13 -> 13, of which waited for: 2 -> 4; matrix products, arithmetic and copies ran while one was open for 7% -> 4% of each run, Pallas kernels for 0% -> 0%
where the time goes in v1:
time: 685 us; the launch traced here: 684 us
  blocking collectives  339 us (49%)
  waiting for transfers between devices  253 us (37%)
  matrix products  24.7 us (4%)
  starting transfers between devices  22.7 us (3%)
  local copies, waits for them, and re-layouts  18.5 us (3%)
  between operations  14.5 us (2%)
  other arithmetic  11 us (2%)
    all_gather x3, blocking collectives, spread(): return lax.all_gather(field, 'tensor', axis=2, tiled=True)  106 us
    all_gather x1, waiting for transfers between devices, per_device(): lax.all_gather(w_conv1, 'seq', axis=1, tiled=True)  99.5 us
    unnamed x7, waiting for transfers between devices  84.4 us
    all_gather x1, blocking collectives, per_device(): lax.all_gather(w_out, 'seq', axis=1, tiled=True)  69.1 us
    all_gather x2, waiting for transfers between devices, norm_back(): lax.all_gather(partial_grad.astype(jnp.bfloat16), 'tensor')  68.3 us
    all_gather x1, blocking collectives, per_device(): lax.all_gather(w_conv2, 'seq', axis=1, tiled=True)  64.2 us
    all_gather x1, blocking collectives, per_device(): lax.all_gather(w_up, 'seq', axis=0, tiled=True)  63.3 us
    all_gather x1, blocking collectives, per_device(): projected_full = lax.all_gather(projected, 'tensor', axis=2, tiled=True)  36.7 us
  transfers between devices with their start and end apart: 13, of which 4 were waited for; matrix products, arithmetic and copies ran while one was open for 4% of the time, Pallas kernels for 0%

profile of v1, /device:TPU:32, one launch (start us, length us, event | category | flops | bytes accessed | tf_op | source)
XLA Modules:
  0.0 683.7 jit_solution(13342523825245579863)
XLA Ops:
  7.2 69.1 %all_gather.37 = bf16[192,1536]{0,1:T(8,128)(2,1)S(1)} all-gather(bf16[192,24]{0,1:T(8,128)(2,1)} %param.10), channel_id=1, replica_groups=mesh['seq'=64,'tensor'=8] {'seq'}, dimensions={1}, use_global_device_ids=true | all-gather | bytes 599040 | tf_op jit(solution)/shard_map/all_gather | solution.py:88
  77.3 1.1 reshape.68
  79.2 5.0 collective-permute-start.4
  84.2 1.9 collective-permute-start.5
  86.1 64.2 %all_gather.43 = bf16[5,768,96]{2,0,1:T(8,128)(2,1)S(1)} all-gather(bf16[5,12,96]{2,0,1:T(8,128)(2,1)S(1)} %copy.52), channel_id=1, replica_groups=mesh['seq'=64,'tensor'=8] {'seq'}, dimensions={1}, use_global_device_ids=true | all-gather | bytes 748800 | tf_op jit(solution)/shard_map/all_gather | solution.py:90
  150.3 2.1 fusion.107
  153.6 1.8 copy.76
  157.1 1.3 fusion.69
  158.8 1.3 fusion.4
  160.1 1.1 fusion.5
  162.8 63.3 %all_gather.41 = bf16[1536,2,96]{2,0,1:T(8,128)(2,1)S(1)} all-gather(bf16[24,2,96]{2,0,1:T(8,128)(2,1)S(1)} %copy.46), channel_id=1, replica_groups=mesh['seq'=64,'tensor'=8] {'seq'}, dimensions={0}, use_global_device_ids=true | all-gather | bytes 599040 | tf_op jit(solution)/shard_map/all_gather | solution.py:89
  226.4 0.9 reshape.69
  228.0 36.7 %all_gather.38 = bf16[2,64,1536]{1,0,2:T(2,128)(2,1)S(1)} all-gather(bf16[2,64,192]{1,0,2:T(2,128)(2,1)S(1)} %bitcast.98), channel_id=1, replica_groups=mesh['seq'=64,'tensor'=8] {'tensor'}, dimensions={2}, use_global_device_ids=true | all-gather | bytes 442368 | tf_op jit(solution)/shard_map/all_gather | solution.py:96
  265.4 1.1 multiply_convert_fusion.1
  267.1 1.9 collective-permute-start
  269.1 3.6 collective-permute-start.1
  272.8 2.4 reduce_sum.65
  275.2 99.5 %all-gather.6.cloned.1.call-done = bf16[5,1536,192]{2,1,0:T(8,128)(2,1)} async-done(((bf16[5,24,192]{2,1,0:T(8,128)(2,1)}), bf16[5,1536,192]{2,1,0:T(8,128)(2,1)}) %all-gather.6.cloned.1.call-update) | async-done | bytes 2949136 | tf_op jit(solution)/shard_map/all_gather | solution.py:101
  374.7 1.4 fusion.43
  376.2 1.4 fusion.41
  377.6 1.4 fusion.45
  379.0 1.4 fusion.6
  380.5 2.1 fusion.9
  382.6 1.0 copy.45
  383.5 35.5 %all_gather.40 = bf16[2,64,1536]{1,0,2:T(2,128)(2,1)S(1)} all-gather(bf16[2,64,192]{1,0,2:T(2,128)(2,1)S(1)} %copy.45), channel_id=1, replica_groups=mesh['seq'=64,'tensor'=8] {'tensor'}, dimensions={2}, use_global_device_ids=true | all-gather | bytes 442368 | tf_op jit(solution)/shard_map/all_gather | solution.py:49
  419.6 0.8 add_convert_fusion
  420.5 34.7 %all_gather.42 = bf16[2,128,768]{1,0,2:T(2,128)(2,1)S(1)} all-gather(bf16[2,128,96]{1,0,2:T(2,128)(2,1)S(1)} %copy.50), channel_id=1, replica_groups=mesh['seq'=64,'tensor'=8] {'tensor'}, dimensions={2}, use_global_device_ids=true | all-gather | bytes 442368 | tf_op jit(solution)/shard_map/all_gather | solution.py:49
  455.8 1.6 multiply_reduce_fusion.1
  457.4 1.1 fusion.75
  460.0 1.1 reshape.70
  461.1 83.6 %reduce-scatter.9.cloned.1.call-done = bf16[192,128]{1,0:T(8,128)(2,1)} async-done(((bf16[1536,128]{1,0:T(8,128)(2,1)}), bf16[192,128]{1,0:T(8,128)(2,1)}) %reduce-scatter.9.cloned.1.call-update) | async-done | bytes 49168
  544.8 0.9 reshape.71
  545.8 1.9 collective-permute-start.6
  547.7 2.6 collective-permute-start.7
  550.3 1.5 fusion.42
  551.8 1.5 fusion.40
  553.4 1.5 fusion.44
  554.9 1.6 fusion
  556.6 2.3 fusion.2
  559.0 3.1 collective-permute-start.2
  563.2 2.4 collective-permute-start.3
  565.9 1.0 collective-permute-done.3
  567.6 0.9 fusion.13
  568.5 68.3 %all-gather.10.cloned.1.call-done = bf16[16,64,1536]{2,1,0:T(8,128)(2,1)} async-done(((bf16[2,64,1536]{2,1,0:T(8,128)(2,1)}), bf16[16,64,1536]{2,1,0:T(8,128)(2,1)}) %all-gather.10.cloned.1.call-update) | async-done | bytes 3145744 | tf_op jit(solution)/shard_map/all_gather | solution.py:70
  636.8 2.4 reduce_sum.80
  639.2 1.0 multiply_reduce_fusion
  640.5 35.6 %all_gather.48 = bf16[2,64,1536]{1,0,2:T(2,128)(2,1)S(1)} all-gather(bf16[2,64,192]{1,0,2:T(2,128)(2,1)S(1)} %copy.60), channel_id=1, replica_groups=mesh['seq'=64,'tensor'=8] {'tensor'}, dimensions={2}, use_global_device_ids=true | all-gather | bytes 442368 | tf_op jit(solution)/shard_map/all_gather | solution.py:49
  676.1 1.1 convolution_convert_fusion.2
  (105 shorter events, 14.1 us)
Async XLA Ops:
  7.2 69.1 %copy-start = (bf16[2,64,192]{2,1,0:T(8,128)(2,1)S(1)}, bf16[2,64,192]{2,1,0:T(8,128)(2,1)}, u32[]{:S(2)}) copy-start(bf16[2,64,192]{2,1,0:T(8,128)(2,1)} %param.9) | copy-start | bytes 147460
  7.2 71.3 %copy-start.1 = (bf16[2,128,96]{1,2,0:T(8,128)(2,1)S(1)}, bf16[2,128,96]{1,2,0:T(8,128)(2,1)}, u32[]{:S(2)}) copy-start(bf16[2,128,96]{1,2,0:T(8,128)(2,1)} %param.17) | copy-start | bytes 147460
  7.2 78.9 %copy-start.15 = (bf16[5,12,96]{2,1,0:T(8,128)(2,1)S(1)}, bf16[5,12,96]{2,1,0:T(8,128)(2,1)}, u32[]{:S(2)}) copy-start(bf16[5,12,96]{2,1,0:T(8,128)(2,1)} %param.16) | copy-start | bytes 34564
  7.2 219.2 %reduce-scatter.7.cloned.1.call-start = ((), (), s32[]{:S(2)}) async-start(), calls=%async_computation.5 | async-start | bytes 442368
  78.4 194.3 %all-gather.8.cloned.1.call-start = ((), (), s32[]{:S(2)}) async-start(), calls=%async_computation.3 | async-start | bytes 3538944 | tf_op jit(solution)/shard_map/all_gather | solution.py:70
  79.2 77.3 %collective-permute-start.4 = (bf16[2,2,96]{1,2,0:T(8,128)(2,1)}, bf16[2,2,96]{1,2,0:T(8,128)(2,1)S(1)}, u32[]{:S(2)}, u32[]{:S(2)}) collective-permute-start(bf16[2,2,96]{1,2,0:T(8,128)(2,1)} %get-tuple-element.28), channel_id=1, source_target_pairs={{8,0},{16,8},{24,16},{32,24},{40,32},{48,40},{56,48},{64,56},{72,6... | collective-permute-start | bytes 2312 | tf_op jit(solution)/shard_map/ppermute | solution.py:19
  84.2 74.3 %collective-permute-start.5 = (bf16[2,2,96]{1,2,0:T(8,128)(2,1)}, bf16[2,2,96]{1,2,0:T(8,128)(2,1)S(1)}, u32[]{:S(2)}, u32[]{:S(2)}) collective-permute-start(bf16[2,2,96]{1,2,0:T(8,128)(2,1)} %get-tuple-element.29), channel_id=1, source_target_pairs={{0,8},{8,16},{16,24},{24,32},{32,40},{40,48},{48,56},{56,64},{64,7... | collective-permute-start | bytes 2312 | tf_op jit(solution)/shard_map/ppermute | solution.py:18
  155.8 5.5 copy-start.2
  156.1 5.9 copy-start.8
  156.1 6.7 copy-start.18
  156.4 69.6 %copy-start.4 = (bf16[1,768,96]{1,2,0:T(8,128)(2,1)}, bf16[1,768,96]{1,2,0:T(8,128)(2,1)S(1)}, u32[]{:S(2)}) copy-start(bf16[1,768,96]{1,2,0:T(8,128)(2,1)S(1)} %copy.78) | copy-start | bytes 442372
  161.3 213.5 %all-gather.6.cloned.1.call-start = ((), (), s32[]{:S(2)}) async-start(), calls=%async_computation.2 | async-start | bytes 3993600 | tf_op jit(solution)/shard_map/all_gather | solution.py:101
  162.0 382.8 %reduce-scatter.9.cloned.1.call-start = ((), (), s32[]{:S(2)}) async-start(), calls=%async_computation.6 | async-start | bytes 442368
  265.4 7.3 %copy-start.19 = (f32[2,64]{1,0:T(2,128)}, f32[2,64]{1,0:T(2,128)S(1)}, u32[]{:S(2)}) copy-start(f32[2,64]{1,0:T(2,128)S(1)} %multiply_reduce_fusion.3) | copy-start | bytes 1540
  265.4 7.3 %copy-start.16 = (f32[2,64]{1,0:T(2,128)}, f32[2,64]{1,0:T(2,128)S(1)}, u32[]{:S(2)}) copy-start(f32[2,64]{1,0:T(2,128)S(1)} %fusion.89) | copy-start | bytes 1540
  267.1 109.0 %collective-permute-start = (bf16[2,2,1536]{2,1,0:T(2,128)(2,1)}, bf16[2,2,1536]{2,1,0:T(2,128)(2,1)}, u32[]{:S(2)}, u32[]{:S(2)}) collective-permute-start(bf16[2,2,1536]{2,1,0:T(2,128)(2,1)} %get-tuple-element.24), channel_id=1, source_target_pairs={{0,8},{8,16},{16,24},{24,32},{32,40},{40,48},{48,56},{56,64},{64,7... | collective-permute-start | bytes 36872 | tf_op jit(solution)/shard_map/ppermute | solution.py:18
  269.1 108.5 %collective-permute-start.1 = (bf16[2,2,1536]{2,1,0:T(2,128)(2,1)}, bf16[2,2,1536]{2,1,0:T(2,128)(2,1)}, u32[]{:S(2)}, u32[]{:S(2)}) collective-permute-start(bf16[2,2,1536]{2,1,0:T(2,128)(2,1)} %get-tuple-element.25), channel_id=1, source_target_pairs={{8,0},{16,8},{24,16},{32,24},{40,32},{48,40},{56,48},{64,56},{72,6... | collective-permute-start | bytes 36872 | tf_op jit(solution)/shard_map/ppermute | solution.py:19
  374.7 5.8 copy-start.13
  420.4 35.4 %copy-start.11 = (bf16[2,128,96]{1,2,0:T(8,128)(2,1)}, bf16[2,128,96]{1,2,0:T(8,128)(2,1)S(1)}, u32[]{:S(2)}) copy-start(bf16[2,128,96]{1,2,0:T(8,128)(2,1)S(1)} %add_convert_fusion) | copy-start | bytes 147460
  458.5 0.6 copy-start.6
  461.1 175.7 %all-gather.10.cloned.1.call-start = ((), (), s32[]{:S(2)}) async-start(), calls=%async_computation.4 | async-start | bytes 3538944 | tf_op jit(solution)/shard_map/all_gather | solution.py:70
  545.8 6.1 collective-permute-start.6
  547.7 5.7 collective-permute-start.7
  554.9 7.5 %copy-start.7 = (bf16[2,128,96]{2,1,0:T(8,128)(2,1)S(1)}, bf16[2,128,96]{2,1,0:T(8,128)(2,1)}, u32[]{:S(2)}) copy-start(bf16[2,128,96]{2,1,0:T(8,128)(2,1)} %copy-done.6) | copy-start | bytes 147460
  554.9 10.7 %copy-start.10 = (bf16[1,768,96]{1,2,0:T(8,128)(2,1)S(1)}, bf16[1,768,96]{1,2,0:T(8,128)(2,1)}, u32[]{:S(2)}) copy-start(bf16[1,768,96]{1,2,0:T(8,128)(2,1)} %copy.76) | copy-start | bytes 442372
  554.9 12.0 %copy-start.9 = (bf16[1,768,96]{1,2,0:T(8,128)(2,1)S(1)}, bf16[1,768,96]{1,2,0:T(8,128)(2,1)}, u32[]{:S(2)}) copy-start(bf16[1,768,96]{1,2,0:T(8,128)(2,1)} %copy-done.8) | copy-start | bytes 442372
  556.5 10.7 %copy-start.3 = (bf16[1,768,96]{1,2,0:T(8,128)(2,1)S(1)}, bf16[1,768,96]{1,2,0:T(8,128)(2,1)}, u32[]{:S(2)}) copy-start(bf16[1,768,96]{1,2,0:T(8,128)(2,1)} %copy-done.2) | copy-start | bytes 442372
  556.5 11.0 %copy-start.5 = (bf16[1,768,96]{1,2,0:T(8,128)(2,1)S(1)}, bf16[1,768,96]{1,2,0:T(8,128)(2,1)}, u32[]{:S(2)}) copy-start(bf16[1,768,96]{1,2,0:T(8,128)(2,1)} %copy-done.4) | copy-start | bytes 442372
  556.5 11.0 %copy-start.12 = (bf16[2,128,96]{1,2,0:T(8,128)(2,1)S(1)}, bf16[2,128,96]{1,2,0:T(8,128)(2,1)}, u32[]{:S(2)}) copy-start(bf16[2,128,96]{1,2,0:T(8,128)(2,1)} %copy-done.11) | copy-start | bytes 147460
  559.0 6.6 collective-permute-start.2
  562.4 76.8 %copy-start.14 = (f32[1536]{0:T(1024)S(1)}, f32[1536]{0:T(1024)}, u32[]{:S(2)}) copy-start(f32[1536]{0:T(1024)} %param.11) | copy-start | bytes 18436
  562.4 76.8 %copy-start.17 = (f32[2,64]{1,0:T(2,128)S(1)}, f32[2,64]{1,0:T(2,128)}, u32[]{:S(2)}) copy-start(f32[2,64]{1,0:T(2,128)} %copy-done.16) | copy-start | bytes 1540
  563.2 3.8 collective-permute-start.3
  567.2 73.0 %copy-start.20 = (f32[2,64]{1,0:T(2,128)S(1)}, f32[2,64]{1,0:T(2,128)}, u32[]{:S(2)}) copy-start(f32[2,64]{1,0:T(2,128)} %copy-done.19) | copy-start | bytes 1540
Sparse Core Ops, SparseCore 0:
  78.5 80.6 reduce-scatter.6
  162.4 78.1 all-gather.7
  242.7 131.9 all-gather.5
  461.2 83.4 reduce-scatter.8
  559.0 77.7 all-gather.9
